TPU v7x, 32 devices: a whole 2x2x4 slice. The times are simulated.
32 devices in a mesh: dp: 4 (over y, core), tensor: 8 (over z, x).
Axes of the slice: x: 2, y: 2, z: 4, core: 2. Of those that a mesh axis runs over, the one named last changes fastest.
Arguments:
- inputs: bfloat16 [16384, 28672], P('dp', 'tensor'), may hold values from -6 to 6
- out_grads: bfloat16 [16384, 8192], P('dp', 'tensor'), may hold values from -6 to 6
- proj_in: bfloat16 [28672, 64], P('tensor'), may hold values from -0.03125 to 0.03125
- proj_out: bfloat16 [8192, 64], P('tensor'), may hold values from -0.0625 to 0.0625
- lengths: int32 [16], replicated, may hold values from 1 to 4096, 16384 in all
- valid_feats: bfloat16 [4096, 4096], P('dp', 'tensor'), may hold values from -6 to 6
Outputs:
- scores: float32 [16, 4096], P(None, ('dp', 'tensor'))
Inputs may be any that keep to these rules, and one draw needn't show every extreme that they name: The lengths sum to 16384; the largest is exactly 4096.
All inputs are finite; a program needn't handle non-finite values.
Results may differ from a plain program's by a relative error of at most 0.003.
Values sent between devices are 32-bit elements; how exact they have to be, the bound alone decides.
No kernel may reach another device: no remote copies, remote signals or barrier semaphores. Data moves between devices by JAX's collectives and lax.ppermute only.
A program may use at most 128 MiB of HBM per device.

v0:
```python
import jax
import jax.numpy as jnp
from jax import lax
from jax.sharding import PartitionSpec as P


def member_rows(positions, prompt_starts, prompt_ends):
    inside = (positions[None, :] >= prompt_starts[:, None]) & (
        positions[None, :] < prompt_ends[:, None]
    )
    return inside.astype(jnp.float32)


def outer_sums(members, grad_rows, act_rows):
    return jnp.einsum(
        "pt,ti,tj->pij", members, grad_rows, act_rows, precision=lax.Precision.HIGHEST
    )


def shards(inputs, out_grads, proj_in, proj_out, lengths, valid_feats):
    tok_rows = inputs.shape[0]
    proj_rank = proj_in.shape[1]
    prompt_count = lengths.shape[0]
    act_part = jnp.dot(inputs, proj_in, preferred_element_type=jnp.float32)
    grad_part = jnp.dot(out_grads, proj_out, preferred_element_type=jnp.float32)
    paired = jnp.concatenate([act_part, grad_part], axis=1)
    prompt_ends = jnp.cumsum(lengths)
    prompt_starts = prompt_ends - lengths
    tensor_count = lax.axis_size("tensor")
    tensor_pos = lax.axis_index("tensor")
    slice_width = proj_rank * proj_rank // tensor_count
    first_row = lax.axis_index("dp") * tok_rows
    summed_pair = lax.psum(paired, "tensor")
    row_count = proj_rank // tensor_count
    grad_rows = lax.dynamic_slice_in_dim(
        summed_pair[:, proj_rank:], tensor_pos * row_count, row_count, 1
    )
    positions = first_row + jnp.arange(tok_rows, dtype=jnp.int32)
    members = member_rows(positions, prompt_starts, prompt_ends)
    gram_rows = outer_sums(members, grad_rows, summed_pair[:, :proj_rank])
    gram_rows = gram_rows.reshape(prompt_count, slice_width)
    summed = lax.psum(gram_rows, "dp")
    features = (summed / lengths[:, None].astype(jnp.float32)).astype(jnp.bfloat16)
    partial_value = lax.dot_general(
        features, valid_feats, (((1,), (1,)), ((), ())), preferred_element_type=jnp.float32
    )
    return lax.psum_scatter(partial_value, "tensor", scatter_dimension=1, tiled=True)


def solution(mesh):
    return jax.shard_map(
        shards,
        mesh=mesh,
        in_specs=(
            P("dp", "tensor"),
            P("dp", "tensor"),
            P("tensor", None),
            P("tensor", None),
            P(),
            P("dp", "tensor"),
        ),
        out_specs=P(None, ("dp", "tensor")),
        check_vma=False,
    )
```

profile of v0, /device:TPU:0, one launch (start us, length us, event | category | flops | bytes accessed | tf_op | source)
XLA Modules:
  0.0 210.4 jit_solution(1678884307394974821)
XLA Ops:
  6.5 0.0 copy-start
  6.5 0.0 copy-start.1
  6.5 0.0 all-reduce.2.cloned.1.call-start
  6.5 6.2 %fusion.11 = f32[4096,64]{0,1:T(8,128)S(1)} fusion(bf16[4096,1024]{1,0:T(8,128)(2,1)} %param.7, bf16[1024,64]{0,1:T(8,128)(2,1)} %param.9), kind=kOutput, calls=%fused_computation.15 | convolution fusion | flops 536870912 | bytes 9568256 | tf_op jit(solution)/shard_map/dot_general | solution.py:25
  12.7 0.0 copy-done.1
  12.7 14.2 %fusion.10 = f32[4096,64]{0,1:T(8,128)S(1)} fusion(bf16[4096,3584]{1,0:T(8,128)(2,1)} %param.6, bf16[3584,64]{0,1:T(8,128)(2,1)S(1)} %copy-done.1), kind=kOutput, calls=%fused_computation.14 | convolution fusion | flops 1879048192 | bytes 30867456 | tf_op jit(solution)/shard_map/dot_general | solution.py:24
  26.9 1.4 pad_maximum_fusion
  28.3 0.0 copy-start.2
  28.3 0.0 all-reduce.2.cloned.1.call-update
  28.4 0.0 reduce-scatter.2.cloned.1.call-start
  28.4 0.6 copy-done.2
  29.0 0.1 copy.8
  29.1 0.1 reduce
  29.3 0.1 convert_bitcast_fusion
  29.4 104.2 %all-reduce.2.cloned.1.call-done = f32[4096,128]{0,1:T(8,128)} async-done(((f32[4096,128]{0,1:T(8,128)}), f32[4096,128]{0,1:T(8,128)}) %all-reduce.2.cloned.1.call-update) | async-done | bytes 2097168 | tf_op jit(solution)/shard_map/psum | solution.py:33
  133.6 0.0 slice-start
  133.6 1.2 slice-done
  134.8 3.0 %fusion.2 = f32[16,8,64]{2,0,1:T(8,128)S(1)} fusion(f32[4096,128]{0,1:T(8,128)} %all-reduce.2.cloned.1.call-done, f32[4096,16]{0,1:T(8,128)S(1)} %convert_bitcast_fusion, f32[4096,8]{0,1:T(8,128)S(1)} %constant_dynamic-slice_fusion), kind=kOutput, calls=%fused_computation.3 | convolution fusion | flops 403177472 | bytes 1474560 | tf_op jit(solution)/shard_map/pt,ti,tj->pij/dot_general | solution.py:15
  137.8 0.1 reshape.34
  137.9 10.6 %psum.15 = f32[16,512]{1,0:T(8,128)S(1)} all-reduce(f32[16,512]{1,0:T(8,128)S(1)} %reshape.34), channel_id=1, replica_groups=mesh['dp'=4,'tensor'=8] {'dp'}, use_global_device_ids=true, to_apply=%region_2.3 | all-reduce | flops 8192 | bytes 65536 | tf_op jit(solution)/shard_map/psum | solution.py:42
  148.6 0.0 copy-done
  148.6 1.0 fusion.7
  149.6 0.0 reduce-scatter.2.cloned.1.call-update
  149.6 54.0 %reduce-scatter.2.cloned.1.call-done = f32[16,128]{1,0:T(8,128)} async-done(((f32[16,1024]{1,0:T(8,128)}), f32[16,128]{1,0:T(8,128)}) %reduce-scatter.2.cloned.1.call-update) | async-done | bytes 8208 | tf_op jit(solution)/shard_map/reduce_scatter | solution.py:47
  (5 shorter events, 0.1 us)
Async XLA Ops:
  6.5 142.0 %copy-start = (bf16[1024,512]{1,0:T(8,128)(2,1)S(1)}, bf16[1024,512]{1,0:T(8,128)(2,1)}, u32[]{:S(2)}) copy-start(bf16[1024,512]{1,0:T(8,128)(2,1)} %param.11) | copy-start | bytes 3145732
  6.5 6.2 %copy-start.1 = (bf16[3584,64]{0,1:T(8,128)(2,1)S(1)}, bf16[3584,64]{0,1:T(8,128)(2,1)}, u32[]{:S(2)}) copy-start(bf16[3584,64]{0,1:T(8,128)(2,1)} %param.8) | copy-start | bytes 1376260
  6.5 127.0 %all-reduce.2.cloned.1.call-start = ((), (), s32[]{:S(2)}) async-start(), calls=%async_computation.1 | async-start | bytes 4194304 | tf_op jit(solution)/shard_map/psum | solution.py:33
  28.3 0.7 copy-start.2
  28.4 175.2 %reduce-scatter.2.cloned.1.call-start = ((), (), s32[]{:S(2)}) async-start(), calls=%async_computation.2 | async-start | bytes 73728 | tf_op jit(solution)/shard_map/reduce_scatter | solution.py:47
  133.6 1.2 slice-start
Sparse Core Ops, SparseCore 0:
  28.5 105.0 all-reduce.1
  149.7 53.7 reduce-scatter.1
where the time goes:
time: 211 us; the launch traced here: 210 us
  waiting for transfers between devices  158 us (75%)
  matrix products  24.4 us (12%)
  between operations  13.5 us (6%)
  blocking collectives  10.6 us (5%)
    psum x1, waiting for transfers between devices, shards(): summed_pair = lax.psum(paired, 'tensor')  104 us
    reduce_scatter x1, waiting for transfers between devices, shards(): lax.psum_scatter(partial_value, 'tensor', scatter_dimension=1, tiled=True)  54 us
    dot_general x1, matrix products, shards(): act_part = jnp.dot(inputs, proj_in, preferred_element_type=jnp.float32)  14.2 us
    psum x1, blocking collectives, shards(): summed = lax.psum(gram_rows, 'dp')  10.6 us
    dot_general x1, matrix products, shards(): grad_part = jnp.dot(out_grads, proj_out, preferred_element_type=jnp.float32)  6.15 us
  transfers between devices with their start and end apart: 2, of which 2 were waited for; matrix products, arithmetic and copies ran while one was open for 0% of the time, Pallas kernels for 0%

commit v1 on v0

--- a/solution.py
+++ b/solution.py
@@ -30,7 +30,11 @@
     tensor_pos = lax.axis_index("tensor")
     slice_width = proj_rank * proj_rank // tensor_count
     first_row = lax.axis_index("dp") * tok_rows
-    summed_pair = lax.psum(paired, "tensor")
+    summed_pair = paired
+    for hop in (1, 2, 4):
+        summed_pair = summed_pair + lax.ppermute(
+            summed_pair, "tensor", [(dev, dev ^ hop) for dev in range(8)]
+        )
     row_count = proj_rank // tensor_count
     grad_rows = lax.dynamic_slice_in_dim(
         summed_pair[:, proj_rank:], tensor_pos * row_count, row_count, 1

time: 211 us -> 290 us (1.37)
  waiting for transfers between devices: 158 us -> 236 us
  starting transfers between devices: 0.04 us -> 7.55 us
  matrix products: 24.4 us -> 19.8 us
    ppermute x0 -> x3, waiting for transfers between devices: none -> 180 us  [shards(): lax.ppermute(summed_pair, 'tensor', [(dev, dev ^ hop) for dev in range(8)])]
    psum x1 -> x0, waiting for transfers between devices: 104 us -> none  [shards(): summed_pair = lax.psum(paired, 'tensor')]
    ppermute x0 -> x3, starting transfers between devices: none -> 7.55 us  [shards(): lax.ppermute(summed_pair, 'tensor', [(dev, dev ^ hop) for dev in range(8)])]
    dot_general x1, matrix products: 6.15 us -> 2.66 us  [shards(): grad_part = jnp.dot(out_grads, proj_out, preferred_element_type=jnp.float32)]
  transfers between devices with their start and end apart: 2 -> 4, of which waited for: 2 -> 4; matrix products, arithmetic and copies ran while one was open for 0% -> 0% of each run, Pallas kernels for 0% -> 0%
where the time goes in v1:
time: 290 us
  waiting for transfers between devices  236 us (81%)
  matrix products  19.8 us (7%)
  between operations  13.5 us (5%)
  blocking collectives  10.3 us (4%)
  starting transfers between devices  7.55 us (3%)
    ppermute x3, waiting for transfers between devices, shards(): lax.ppermute(summed_pair, 'tensor', [(dev, dev ^ hop) for dev in range(8)])  180 us
    reduce_scatter x1, waiting for transfers between devices, shards(): lax.psum_scatter(partial_value, 'tensor', scatter_dimension=1, tiled=True)  56 us
    dot_general x1, matrix products, shards(): act_part = jnp.dot(inputs, proj_in, preferred_element_type=jnp.float32)  14.4 us
    psum x1, blocking collectives, shards(): summed = lax.psum(gram_rows, 'dp')  10.3 us
    ppermute x3, starting transfers between devices, shards(): lax.ppermute(summed_pair, 'tensor', [(dev, dev ^ hop) for dev in range(8)])  7.55 us
  transfers between devices with their start and end apart: 4, of which 4 were waited for; matrix products, arithmetic and copies ran while one was open for 0% of the time, Pallas kernels for 0%

profile of v1, /device:TPU:0, one launch (start us, length us, event | category | flops | bytes accessed | tf_op | source)
XLA Modules:
  0.0 289.7 jit_solution(18234952908170459080)
XLA Ops:
  6.5 0.0 copy-start
  6.5 0.0 copy-start.2
  6.5 0.0 reduce-scatter.2.cloned.1.call-start
  6.5 0.0 copy-start.1
  6.5 14.4 %fusion.11 = f32[4096,64]{0,1:T(8,128)S(1)} fusion(bf16[4096,3584]{1,0:T(8,128)(2,1)} %param.6, bf16[3584,64]{0,1:T(8,128)(2,1)} %param.8), kind=kOutput, calls=%fused_computation.15 | convolution fusion | flops 1879048192 | bytes 30867456 | tf_op jit(solution)/shard_map/dot_general | solution.py:24
  20.9 0.0 copy-done.2
  20.9 0.0 copy-done.1
  20.9 2.7 fusion.12
  23.6 0.2 pad_maximum_fusion
  23.8 3.0 %collective-permute-start = (f32[4096,128]{0,1:T(8,128)S(1)}, f32[4096,128]{0,1:T(8,128)S(1)}, u32[]{:S(2)}, u32[]{:S(2)}) collective-permute-start(f32[4096,128]{0,1:T(8,128)S(1)} %pad_maximum_fusion), channel_id=1, source_target_pairs={{0,1},{1,0},{2,3},{3,2},{4,5},{5,4},{6,7},{7,6},{8,9},{9,8},{10,11... | collective-permute-start | bytes 6291464 | tf_op jit(solution)/shard_map/ppermute | solution.py:35
  26.8 45.6 %collective-permute-done = f32[4096,128]{0,1:T(8,128)S(1)} collective-permute-done((f32[4096,128]{0,1:T(8,128)S(1)}, f32[4096,128]{0,1:T(8,128)S(1)}, u32[]{:S(2)}, u32[]{:S(2)}) %collective-permute-start) | collective-permute-done | bytes 2097184 | tf_op jit(solution)/shard_map/ppermute | solution.py:35
  72.4 0.2 fusion.9
  72.7 0.0 copy-start.3
  72.7 1.9 collective-permute-start.1
  74.6 45.0 %collective-permute-done.1 = f32[4096,128]{0,1:T(8,128)S(1)} collective-permute-done((f32[4096,128]{0,1:T(8,128)S(1)}, f32[4096,128]{0,1:T(8,128)S(1)}, u32[]{:S(2)}, u32[]{:S(2)}) %collective-permute-start.1) | collective-permute-done | bytes 2097184 | tf_op jit(solution)/shard_map/ppermute | solution.py:35
  119.5 0.2 add.27
  119.8 2.6 collective-permute-start.2
  122.4 0.0 copy-done.3
  122.4 0.1 copy.8
  122.5 0.1 reduce
  122.7 0.1 convert_bitcast_fusion
  122.8 88.9 %collective-permute-done.2 = f32[4096,128]{0,1:T(8,128)} collective-permute-done((f32[4096,128]{0,1:T(8,128)S(1)}, f32[4096,128]{0,1:T(8,128)}, u32[]{:S(2)}, u32[]{:S(2)}) %collective-permute-start.2) | collective-permute-done | bytes 2097184 | tf_op jit(solution)/shard_map/ppermute | solution.py:35
  211.7 1.8 add.28
  213.5 0.1 slice.8
  213.6 1.8 fusion.2
  215.5 0.1 reshape.34
  215.5 10.3 %psum.7 = f32[16,512]{1,0:T(8,128)S(1)} all-reduce(f32[16,512]{1,0:T(8,128)S(1)} %reshape.34), channel_id=1, replica_groups=mesh['dp'=4,'tensor'=8] {'dp'}, use_global_device_ids=true, to_apply=%region_1.2 | all-reduce | flops 8192 | bytes 65536 | tf_op jit(solution)/shard_map/psum | solution.py:46
  225.8 0.0 copy-done
  225.8 1.0 fusion.7
  226.8 0.0 reduce-scatter.2.cloned.1.call-update
  226.9 56.0 %reduce-scatter.2.cloned.1.call-done = f32[16,128]{1,0:T(8,128)} async-done(((f32[16,1024]{1,0:T(8,128)}), f32[16,128]{1,0:T(8,128)}) %reduce-scatter.2.cloned.1.call-update) | async-done | bytes 8208 | tf_op jit(solution)/shard_map/reduce_scatter | solution.py:51
  (5 shorter events, 0.1 us)
Async XLA Ops:
  6.5 219.3 %copy-start = (bf16[1024,512]{1,0:T(8,128)(2,1)S(1)}, bf16[1024,512]{1,0:T(8,128)(2,1)}, u32[]{:S(2)}) copy-start(bf16[1024,512]{1,0:T(8,128)(2,1)} %param.11) | copy-start | bytes 3145732
  6.5 14.4 %copy-start.2 = (bf16[1024,64]{0,1:T(8,128)(2,1)S(1)}, bf16[1024,64]{0,1:T(8,128)(2,1)}, u32[]{:S(2)}) copy-start(bf16[1024,64]{0,1:T(8,128)(2,1)} %param.9) | copy-start | bytes 393220
  6.5 276.3 %reduce-scatter.2.cloned.1.call-start = ((), (), s32[]{:S(2)}) async-start(), calls=%async_computation.1 | async-start | bytes 73728 | tf_op jit(solution)/shard_map/reduce_scatter | solution.py:51
  6.5 14.4 %copy-start.1 = (bf16[4096,1024]{1,0:T(8,128)(2,1)S(1)}, bf16[4096,1024]{1,0:T(8,128)(2,1)}, u32[]{:S(2)}) copy-start(bf16[4096,1024]{1,0:T(8,128)(2,1)} %param.7) | copy-start | bytes 25165828
  23.8 48.7 %collective-permute-start = (f32[4096,128]{0,1:T(8,128)S(1)}, f32[4096,128]{0,1:T(8,128)S(1)}, u32[]{:S(2)}, u32[]{:S(2)}) collective-permute-start(f32[4096,128]{0,1:T(8,128)S(1)} %pad_maximum_fusion), channel_id=1, source_target_pairs={{0,1},{1,0},{2,3},{3,2},{4,5},{5,4},{6,7},{7,6},{8,9},{9,8},{10,11... | collective-permute-start | bytes 6291464 | tf_op jit(solution)/shard_map/ppermute | solution.py:35
  72.7 49.7 %copy-start.3 = (s32[16]{0:T(128)S(1)}, s32[16]{0:T(128)}, u32[]{:S(2)}) copy-start(s32[16]{0:T(128)} %param.10) | copy-start | bytes 196
  72.7 46.9 %collective-permute-start.1 = (f32[4096,128]{0,1:T(8,128)S(1)}, f32[4096,128]{0,1:T(8,128)S(1)}, u32[]{:S(2)}, u32[]{:S(2)}) collective-permute-start(f32[4096,128]{0,1:T(8,128)S(1)} %fusion.9), channel_id=1, source_target_pairs={{0,2},{1,3},{2,0},{3,1},{4,6},{5,7},{6,4},{7,5},{8,10},{9,11},{10,... | collective-permute-start | bytes 6291464 | tf_op jit(solution)/shard_map/ppermute | solution.py:35
  119.8 91.9 %collective-permute-start.2 = (f32[4096,128]{0,1:T(8,128)S(1)}, f32[4096,128]{0,1:T(8,128)}, u32[]{:S(2)}, u32[]{:S(2)}) collective-permute-start(f32[4096,128]{0,1:T(8,128)S(1)} %add.27), channel_id=1, source_target_pairs={{0,4},{1,5},{2,6},{3,7},{4,0},{5,1},{6,2},{7,3},{8,12},{9,13},{10,... | collective-permute-start | bytes 6291464 | tf_op jit(solution)/shard_map/ppermute | solution.py:35
Sparse Core Ops, SparseCore 0:
  227.0 55.7 reduce-scatter.1
